TPU v7x, 256 devices: a whole 4x4x8 slice. The times are simulated.
256 devices in a mesh: slab: 32 (over z, y), snap: 8 (over x, core).
Axes of the slice: x: 4, y: 4, z: 8, core: 2. Of those that a mesh axis runs over, the one named last changes fastest.
Arguments:
- flow: bfloat16 [128, 3, 64, 64, 128], P('snap', None, 'slab'), may hold values from -127 to 127
- large_scale: bfloat16 [3, 64, 64, 128], P(None, 'slab'), may hold values from -6 to 6
- modulation: float32 [128, 64], replicated, may hold values from -15 to 15
- metric: float32 [4, 64, 64, 128], P(None, 'slab'), may hold values from -0.5 to 9.6
Outputs:
- whitened: float32 [128, 3, 64, 64, 128], P(None, None, 'slab', 'snap')
All inputs are finite; a program needn't handle non-finite values.
Results may differ from a plain program's by a relative error of at most 0.0003.
Values may be sent and summed in bfloat16 or wider, within the bound.
A program may use at most 64 MiB of HBM per device.

v0:
```python
import jax
import jax.numpy as jnp
from jax import lax
from jax.sharding import PartitionSpec as P

NSITER = 6


def with_halo(block, sides, width):
    for axis, dim in sides:
        count = lax.axis_size(axis)
        forward = [(i, i + 1) for i in range(count - 1)]
        backward = [(target, source) for source, target in forward]
        low = lax.ppermute(
            lax.slice_in_dim(block, block.shape[dim] - width, None, axis=dim), axis, forward
        )
        high = lax.ppermute(lax.slice_in_dim(block, 0, width, axis=dim), axis, backward)
        block = jnp.concatenate([low, block, high], axis=dim)
    return block


def vorticity(velocity, metric):
    metric_x = metric[0]
    shear_xy = metric[1]
    metric_y = metric[2]
    metric_z = metric[3]

    def along_x(values):
        return 0.5 * (values[..., 1:-1, 2:, :] - values[..., 1:-1, :-2, :])

    def along_y(values):
        return 0.5 * (values[..., 2:, 1:-1, :] - values[..., :-2, 1:-1, :])

    def along_z(values):
        center = values[..., 1:-1, 1:-1, :]
        return 0.5 * (jnp.roll(center, -1, -1) - jnp.roll(center, 1, -1))

    def slope_x(values):
        return metric_x * along_x(values) + shear_xy * along_y(values)

    def slope_y(values):
        return metric_y * along_y(values)

    def slope_z(values):
        return metric_z * along_z(values)

    stream = velocity[..., 0, :, :, :]
    normal = velocity[..., 1, :, :, :]
    spanwise = velocity[..., 2, :, :, :]
    around_x = slope_y(spanwise) - slope_z(normal)
    around_y = slope_z(stream) - slope_x(spanwise)
    around_z = slope_x(normal) - slope_y(stream)
    return jnp.stack([around_x, around_y, around_z], axis=-4)


def wrap_columns(values):
    return jnp.concatenate([values[..., -1:, :], values, values[..., :1, :]], axis=-2)


def whitening(correlation):
    identity = jnp.eye(correlation.shape[0], dtype=correlation.dtype)
    frob_scale = jnp.sqrt(jnp.sum(correlation * correlation) + 1e-06)
    approx = correlation / frob_scale
    inverse = identity
    for repeat in range(NSITER):
        factor = 0.5 * (3.0 * identity - jnp.dot(inverse, approx, precision=lax.Precision.HIGHEST))
        approx = jnp.dot(approx, factor, precision=lax.Precision.HIGHEST)
        inverse = jnp.dot(factor, inverse, precision=lax.Precision.HIGHEST)
    return inverse / jnp.sqrt(frob_scale)


def inner_rows(left_rows, right_rows):
    return lax.dot_general(
        left_rows,
        right_rows,
        (((1,), (1,)), ((), ())),
        precision=lax.Precision.HIGHEST,
        preferred_element_type=jnp.float32,
    )


def planes_padded(flow, large_scale):
    joined = jnp.concatenate([flow, large_scale[None]], axis=0)
    return with_halo(joined, (("slab", 2),), 1)


def per_device(flow, large_scale, modulation, metric):
    snap_count = lax.axis_size("snap")
    slab_count = lax.axis_size("slab")
    own_snaps = flow.shape[0]
    block_cols = flow.shape[3] // snap_count
    snap_index = lax.axis_index("snap")
    mod_ext = jnp.concatenate([modulation[:, -1:], modulation, modulation[:, :1]], axis=1)
    padded = planes_padded(flow, large_scale)
    large_ext = wrap_columns(padded[own_snaps].astype(jnp.float32))
    mod_mine = lax.dynamic_slice_in_dim(mod_ext, snap_index * own_snaps, own_snaps, 0)
    velocity = (
        wrap_columns(padded[:own_snaps].astype(jnp.float32))
        + mod_mine[:, None, None, :, None] * large_ext[None]
    )
    local_fields = vorticity(velocity, metric)
    pieces = local_fields.reshape(
        own_snaps, 3, local_fields.shape[2], snap_count, block_cols, local_fields.shape[4]
    )
    fields = lax.all_to_all(pieces, "snap", split_axis=3, concat_axis=0, tiled=True)[:, :, :, 0]
    snapshot_rows = fields.reshape(fields.shape[0], -1)
    gram_local = inner_rows(snapshot_rows, snapshot_rows)
    gram_total = lax.psum(gram_local, ("slab", "snap"))
    correlation = gram_total / (snapshot_rows.shape[1] * slab_count * snap_count)
    weights = whitening(correlation)
    result = jnp.dot(weights, snapshot_rows, precision=lax.Precision.HIGHEST)
    return result.reshape(fields.shape)


def solution(mesh):
    return jax.shard_map(
        per_device,
        mesh=mesh,
        in_specs=(
            P("snap", None, "slab", None, None),
            P(None, "slab", None, None),
            P(),
            P(None, "slab", None, None),
        ),
        out_specs=P(None, None, "slab", "snap", None),
        check_vma=False,
    )
```

profile of v0, /device:TPU:1, one launch (start us, length us, event | category | flops | bytes accessed | tf_op | source)
XLA Modules:
  0.0 358.1 jit_solution(2387422955889473556)
XLA Ops:
  6.5 0.0 copy-start
  6.5 0.0 copy-start.2
  6.5 0.0 copy-start.3
  6.5 0.0 all-reduce.2.cloned.1.call-start
  6.5 2.9 fusion.21
  9.4 4.1 %collective-permute-start = (bf16[17,3,1,64,128]{4,3,2,1,0:T(8,128)(2,1)}, bf16[17,3,1,64,128]{4,3,2,1,0:T(8,128)(2,1)S(1)}, u32[]{:S(2)}, u32[]{:S(2)}) collective-permute-start(bf16[17,3,1,64,128]{4,3,2,1,0:T(8,128)(2,1)} %get-tuple-element.20), channel_id=1, source_target_pairs={{0,8},{8,16},{16,24},{24,32},{32,40},{40,48},{48,56},{56,64},{64,7... | collective-permute-start | bytes 2506760 | tf_op jit(solution)/shard_map/ppermute | solution.py:14
  13.5 1.3 collective-permute-start.1
  14.8 0.0 copy-done.3
  14.8 0.1 dynamic-slice_maximum_fusion
  14.9 0.1 copy.10
  15.0 1.0 multiply_bitcast_fusion.2
  15.9 15.1 %collective-permute-done = bf16[17,3,1,64,128]{4,3,2,1,0:T(8,128)(2,1)S(1)} collective-permute-done((bf16[17,3,1,64,128]{4,3,2,1,0:T(8,128)(2,1)}, bf16[17,3,1,64,128]{4,3,2,1,0:T(8,128)(2,1)S(1)}, u32[]{:S(2)}, u32[]{:S(2)}) %collective-permute-start) | collective-permute-done | bytes 835616 | tf_op jit(solution)/shard_map/ppermute | solution.py:14
  31.0 3.8 %collective-permute-done.1 = bf16[17,3,1,64,128]{4,3,2,1,0:T(8,128)(2,1)S(1)} collective-permute-done((bf16[17,3,1,64,128]{4,3,2,1,0:T(8,128)(2,1)}, bf16[17,3,1,64,128]{4,3,2,1,0:T(8,128)(2,1)S(1)}, u32[]{:S(2)}, u32[]{:S(2)}) %collective-permute-start.1) | collective-permute-done | bytes 835616 | tf_op jit(solution)/shard_map/ppermute | solution.py:17
  34.8 0.0 copy-done
  34.8 0.0 copy-done.2
  34.8 0.5 pad_maximum_fusion
  35.3 0.7 slice_convert_fusion
  36.1 0.1 fusion.27
  36.3 1.5 maximum_add_fusion
  37.7 0.5 slice_bitcast_fusion.2
  38.2 0.9 fusion.28
  39.1 0.9 fusion.29
  40.0 0.8 fusion.9
  40.7 1.5 fusion.19
  42.2 0.2 pad_maximum_fusion.1
  42.5 0.3 copy.19
  42.8 43.4 %all_to_all.15 = f32[16,3,2,8,8,128]{5,4,2,1,0,3:T(8,128)} all-to-all(f32[16,3,2,8,8,128]{5,4,2,1,0,3:T(8,128)S(1)} %copy.19), channel_id=1, replica_groups=mesh['slab'=32,'snap'=8] {'snap'}, dimensions={3} | all-to-all | bytes 6291456 | tf_op jit(solution)/shard_map/all_to_all | solution.py:105
  86.2 2.8 reshape_squeeze.3
  89.0 3.2 fusion.34
  92.2 0.0 all-reduce.2.cloned.1.call-update
  92.2 2.4 copy.16
  94.6 0.0 copy-start.1
  94.6 242.7 %all-reduce.2.cloned.1.call-done = f32[128,128]{1,0:T(8,128)} async-done(((f32[128,128]{1,0:T(8,128)}), f32[128,128]{1,0:T(8,128)}) %all-reduce.2.cloned.1.call-update) | async-done | bytes 65552 | tf_op jit(solution)/shard_map/psum | solution.py:108
  337.3 1.5 multiply_reduce_fusion
  339.5 1.0 fusion.6
  340.5 0.2 fusion.23
  340.7 1.0 fusion.24
  341.8 0.2 fusion.5
  342.0 0.2 fusion.36
  342.2 0.2 fusion.35
  342.4 0.2 fusion.4
  342.6 0.2 fusion.38
  342.8 0.2 fusion.37
  343.0 0.2 fusion.3
  343.3 0.2 fusion.40
  343.5 0.2 fusion.39
  343.7 0.2 fusion.2
  343.9 0.2 fusion.41
  344.1 0.2 fusion.42
  344.3 0.2 fusion.1
  344.5 0.2 fusion
  344.7 0.0 copy-done.1
  344.7 3.0 fusion.43
  347.8 3.5 copy.17
  (4 shorter events, 0.1 us)
Async XLA Ops:
  6.5 28.2 %copy-start = (bf16[16,3,2,64,128]{4,3,2,1,0:T(8,128)(2,1)S(1)}, bf16[16,3,2,64,128]{4,3,2,1,0:T(8,128)(2,1)}, u32[]{:S(2)}) copy-start(bf16[16,3,2,64,128]{4,3,2,1,0:T(8,128)(2,1)} %param.4) | copy-start | bytes 4718596
  6.5 28.2 %copy-start.2 = (bf16[3,2,64,128]{3,2,1,0:T(8,128)(2,1)S(1)}, bf16[3,2,64,128]{3,2,1,0:T(8,128)(2,1)}, u32[]{:S(2)}) copy-start(bf16[3,2,64,128]{3,2,1,0:T(8,128)(2,1)} %param.5) | copy-start | bytes 294916
  6.5 8.2 %copy-start.3 = (f32[128,64]{0,1:T(8,128)S(1)}, f32[128,64]{0,1:T(8,128)}, u32[]{:S(2)}) copy-start(f32[128,64]{0,1:T(8,128)} %param.6) | copy-start | bytes 98308
  6.5 330.8 %all-reduce.2.cloned.1.call-start = ((), (), s32[]{:S(2)}) async-start(), calls=%async_computation.1 | async-start | bytes 131072 | tf_op jit(solution)/shard_map/psum | solution.py:108
  9.4 21.6 %collective-permute-start = (bf16[17,3,1,64,128]{4,3,2,1,0:T(8,128)(2,1)}, bf16[17,3,1,64,128]{4,3,2,1,0:T(8,128)(2,1)S(1)}, u32[]{:S(2)}, u32[]{:S(2)}) collective-permute-start(bf16[17,3,1,64,128]{4,3,2,1,0:T(8,128)(2,1)} %get-tuple-element.20), channel_id=1, source_target_pairs={{0,8},{8,16},{16,24},{24,32},{32,40},{40,48},{48,56},{56,64},{64,7... | collective-permute-start | bytes 2506760 | tf_op jit(solution)/shard_map/ppermute | solution.py:14
  13.5 21.3 %collective-permute-start.1 = (bf16[17,3,1,64,128]{4,3,2,1,0:T(8,128)(2,1)}, bf16[17,3,1,64,128]{4,3,2,1,0:T(8,128)(2,1)S(1)}, u32[]{:S(2)}, u32[]{:S(2)}) collective-permute-start(bf16[17,3,1,64,128]{4,3,2,1,0:T(8,128)(2,1)} %get-tuple-element.21), channel_id=1, source_target_pairs={{8,0},{16,8},{24,16},{32,24},{40,32},{48,40},{56,48},{64,56},{72,6... | collective-permute-start | bytes 2506760 | tf_op jit(solution)/shard_map/ppermute | solution.py:17
  94.6 250.2 %copy-start.1 = (f32[6144,128]{1,0:T(8,128)S(1)}, f32[6144,128]{1,0:T(8,128)}, u32[]{:S(2)}) copy-start(f32[6144,128]{1,0:T(8,128)} %copy.16) | copy-start | bytes 9437188
Sparse Core Ops, SparseCore 0:
  92.3 244.9 all-reduce.1
where the time goes:
time: 358 us
  waiting for transfers between devices  262 us (73%)
  blocking collectives  43.4 us (12%)
  between operations  14.4 us (4%)
  local copies, waits for them, and re-layouts  11.3 us (3%)
  matrix products  11.3 us (3%)
  other arithmetic  10.6 us (3%)
  starting transfers between devices  5.35 us (1%)
    psum x1, waiting for transfers between devices, per_device(): gram_total = lax.psum(gram_local, ('slab', 'snap'))  243 us
    all_to_all x1, blocking collectives, per_device(): lax.all_to_all(pieces, 'snap', split_axis=3, concat_axis=0, tiled=True)  43.4 us
    ppermute x1, waiting for transfers between devices, with_halo(): lax.ppermute(lax.slice_in_dim(block, block.shape[dim] - width, None, axis...  15.1 us
  transfers between devices with their start and end apart: 3, of which 3 were waited for; matrix products, arithmetic and copies ran while one was open for 1% of the time, Pallas kernels for 0%

commit v1 on v0

--- a/solution.py
+++ b/solution.py
@@ -105,7 +105,7 @@
     fields = lax.all_to_all(pieces, "snap", split_axis=3, concat_axis=0, tiled=True)[:, :, :, 0]
     snapshot_rows = fields.reshape(fields.shape[0], -1)
     gram_local = inner_rows(snapshot_rows, snapshot_rows)
-    gram_total = lax.psum(gram_local, ("slab", "snap"))
+    gram_total = lax.psum(lax.psum(gram_local, "slab"), "snap")
     correlation = gram_total / (snapshot_rows.shape[1] * slab_count * snap_count)
     weights = whitening(correlation)
     result = jnp.dot(weights, snapshot_rows, precision=lax.Precision.HIGHEST)

time: 358 us -> 323 us (0.902)
  waiting for transfers between devices: 262 us -> 224 us
    psum x1 -> x2, waiting for transfers between devices: 243 us -> 205 us  [per_device(): gram_total = lax.psum(lax.psum(gram_local, 'slab'), 'snap')]
  transfers between devices with their start and end apart: 3 -> 4, of which waited for: 3 -> 4; matrix products, arithmetic and copies ran while one was open for 1% -> 1% of each run, Pallas kernels for 0% -> 0%
where the time goes in v1:
time: 323 us; the launch traced here: 321 us
  waiting for transfers between devices  224 us (69%)
  blocking collectives  43.4 us (13%)
  between operations  14.4 us (4%)
  local copies, waits for them, and re-layouts  11.3 us (3%)
  matrix products  11.3 us (3%)
  other arithmetic  10.6 us (3%)
  starting transfers between devices  5.58 us (2%)
    psum x2, waiting for transfers between devices, per_device(): gram_total = lax.psum(lax.psum(gram_local, 'slab'), 'snap')  205 us
    all_to_all x1, blocking collectives, per_device(): lax.all_to_all(pieces, 'snap', split_axis=3, concat_axis=0, tiled=True)  43.4 us
    ppermute x1, waiting for transfers between devices, with_halo(): lax.ppermute(lax.slice_in_dim(block, block.shape[dim] - width, None, axis...  15.1 us
  transfers between devices with their start and end apart: 4, of which 4 were waited for; matrix products, arithmetic and copies ran while one was open for 1% of the time, Pallas kernels for 0%

profile of v1, /device:TPU:1, one launch (start us, length us, event | category | flops | bytes accessed | tf_op | source)
XLA Modules:
  0.0 321.0 jit_solution(16249024335755964417)
XLA Ops:
  6.5 0.0 copy-start
  6.5 0.0 copy-start.2
  6.5 0.0 copy-start.3
  6.5 0.0 all-reduce.3.cloned.1.call-start
  6.5 2.9 fusion.21
  9.4 4.1 %collective-permute-start = (bf16[17,3,1,64,128]{4,3,2,1,0:T(8,128)(2,1)}, bf16[17,3,1,64,128]{4,3,2,1,0:T(8,128)(2,1)S(1)}, u32[]{:S(2)}, u32[]{:S(2)}) collective-permute-start(bf16[17,3,1,64,128]{4,3,2,1,0:T(8,128)(2,1)} %get-tuple-element.20), channel_id=1, source_target_pairs={{0,8},{8,16},{16,24},{24,32},{32,40},{40,48},{48,56},{56,64},{64,7... | collective-permute-start | bytes 2506760 | tf_op jit(solution)/shard_map/ppermute | solution.py:14
  13.5 1.3 collective-permute-start.1
  14.8 0.0 copy-done.3
  14.8 0.1 dynamic-slice_maximum_fusion
  14.9 0.1 copy.10
  15.0 1.0 multiply_bitcast_fusion.2
  15.9 15.1 %collective-permute-done = bf16[17,3,1,64,128]{4,3,2,1,0:T(8,128)(2,1)S(1)} collective-permute-done((bf16[17,3,1,64,128]{4,3,2,1,0:T(8,128)(2,1)}, bf16[17,3,1,64,128]{4,3,2,1,0:T(8,128)(2,1)S(1)}, u32[]{:S(2)}, u32[]{:S(2)}) %collective-permute-start) | collective-permute-done | bytes 835616 | tf_op jit(solution)/shard_map/ppermute | solution.py:14
  31.0 3.8 %collective-permute-done.1 = bf16[17,3,1,64,128]{4,3,2,1,0:T(8,128)(2,1)S(1)} collective-permute-done((bf16[17,3,1,64,128]{4,3,2,1,0:T(8,128)(2,1)}, bf16[17,3,1,64,128]{4,3,2,1,0:T(8,128)(2,1)S(1)}, u32[]{:S(2)}, u32[]{:S(2)}) %collective-permute-start.1) | collective-permute-done | bytes 835616 | tf_op jit(solution)/shard_map/ppermute | solution.py:17
  34.8 0.0 copy-done
  34.8 0.0 copy-done.2
  34.8 0.5 pad_maximum_fusion
  35.3 0.7 slice_convert_fusion
  36.1 0.1 fusion.27
  36.3 1.5 maximum_add_fusion
  37.7 0.5 slice_bitcast_fusion.2
  38.2 0.9 fusion.28
  39.1 0.9 fusion.29
  40.0 0.8 fusion.9
  40.7 1.5 fusion.19
  42.2 0.2 pad_maximum_fusion.1
  42.5 0.3 copy.19
  42.8 43.4 %all_to_all.15 = f32[16,3,2,8,8,128]{5,4,2,1,0,3:T(8,128)} all-to-all(f32[16,3,2,8,8,128]{5,4,2,1,0,3:T(8,128)S(1)} %copy.19), channel_id=1, replica_groups=mesh['slab'=32,'snap'=8] {'snap'}, dimensions={3} | all-to-all | bytes 6291456 | tf_op jit(solution)/shard_map/all_to_all | solution.py:105
  86.2 2.8 reshape_squeeze.3
  89.0 3.2 %fusion.34 = f32[128,128]{1,0:T(8,128)} fusion(f32[128,6144]{1,0:T(8,128)S(1)} %reshape_squeeze.3), kind=kOutput, calls=%fused_computation.69 | convolution fusion | flops 1207959552 | bytes 3211264 | tf_op jit(solution)/shard_map/dot_general | solution.py:73
  92.2 0.0 all-reduce.3.cloned.1.call-update
  92.2 0.2 all-reduce.5.cloned.1.call-start
  92.4 140.2 %all-reduce.3.cloned.1.call-done = f32[128,128]{1,0:T(8,128)} async-done(((f32[128,128]{1,0:T(8,128)}), f32[128,128]{1,0:T(8,128)}) %all-reduce.3.cloned.1.call-update) | async-done | bytes 65552 | tf_op jit(solution)/shard_map/psum | solution.py:108
  232.7 0.0 all-reduce.5.cloned.1.call-update
  232.7 2.4 copy.16
  235.1 0.0 copy-start.1
  235.1 65.2 %all-reduce.5.cloned.1.call-done = f32[128,128]{1,0:T(8,128)} async-done(((f32[128,128]{1,0:T(8,128)}), f32[128,128]{1,0:T(8,128)}) %all-reduce.5.cloned.1.call-update) | async-done | bytes 65552 | tf_op jit(solution)/shard_map/psum | solution.py:108
  300.2 1.5 multiply_reduce_fusion
  302.4 1.0 fusion.6
  303.5 0.2 fusion.23
  303.6 1.0 fusion.24
  304.7 0.2 fusion.5
  304.9 0.2 fusion.36
  305.1 0.2 fusion.35
  305.3 0.2 fusion.4
  305.5 0.2 fusion.38
  305.8 0.2 fusion.37
  306.0 0.2 fusion.3
  306.2 0.2 fusion.40
  306.4 0.2 fusion.39
  306.6 0.2 fusion.2
  306.8 0.2 fusion.41
  307.0 0.2 fusion.42
  307.2 0.2 fusion.1
  307.4 0.2 fusion
  307.7 0.0 copy-done.1
  307.7 3.0 fusion.43
  310.7 3.5 %copy.17 = f32[128,3,2,8,128]{4,3,2,1,0:T(8,128)} copy(f32[128,3,2,8,128]{4,0,3,2,1:T(8,128)S(1)} %fusion.43) | data formatting | bytes 6291456 | tf_op jit(solution)/shard_map/dot_general | solution.py:111
  (4 shorter events, 0.1 us)
Async XLA Ops:
  6.5 28.2 %copy-start = (bf16[16,3,2,64,128]{4,3,2,1,0:T(8,128)(2,1)S(1)}, bf16[16,3,2,64,128]{4,3,2,1,0:T(8,128)(2,1)}, u32[]{:S(2)}) copy-start(bf16[16,3,2,64,128]{4,3,2,1,0:T(8,128)(2,1)} %param.4) | copy-start | bytes 4718596
  6.5 28.2 %copy-start.2 = (bf16[3,2,64,128]{3,2,1,0:T(8,128)(2,1)S(1)}, bf16[3,2,64,128]{3,2,1,0:T(8,128)(2,1)}, u32[]{:S(2)}) copy-start(bf16[3,2,64,128]{3,2,1,0:T(8,128)(2,1)} %param.5) | copy-start | bytes 294916
  6.5 8.2 %copy-start.3 = (f32[128,64]{0,1:T(8,128)S(1)}, f32[128,64]{0,1:T(8,128)}, u32[]{:S(2)}) copy-start(f32[128,64]{0,1:T(8,128)} %param.6) | copy-start | bytes 98308
  6.5 226.1 %all-reduce.3.cloned.1.call-start = ((), (), s32[]{:S(2)}) async-start(), calls=%async_computation.1 | async-start | bytes 131072 | tf_op jit(solution)/shard_map/psum | solution.py:108
  9.4 21.6 %collective-permute-start = (bf16[17,3,1,64,128]{4,3,2,1,0:T(8,128)(2,1)}, bf16[17,3,1,64,128]{4,3,2,1,0:T(8,128)(2,1)S(1)}, u32[]{:S(2)}, u32[]{:S(2)}) collective-permute-start(bf16[17,3,1,64,128]{4,3,2,1,0:T(8,128)(2,1)} %get-tuple-element.20), channel_id=1, source_target_pairs={{0,8},{8,16},{16,24},{24,32},{32,40},{40,48},{48,56},{56,64},{64,7... | collective-permute-start | bytes 2506760 | tf_op jit(solution)/shard_map/ppermute | solution.py:14
  13.5 21.3 %collective-permute-start.1 = (bf16[17,3,1,64,128]{4,3,2,1,0:T(8,128)(2,1)}, bf16[17,3,1,64,128]{4,3,2,1,0:T(8,128)(2,1)S(1)}, u32[]{:S(2)}, u32[]{:S(2)}) collective-permute-start(bf16[17,3,1,64,128]{4,3,2,1,0:T(8,128)(2,1)} %get-tuple-element.21), channel_id=1, source_target_pairs={{8,0},{16,8},{24,16},{32,24},{40,32},{48,40},{56,48},{64,56},{72,6... | collective-permute-start | bytes 2506760 | tf_op jit(solution)/shard_map/ppermute | solution.py:17
  92.2 208.0 %all-reduce.5.cloned.1.call-start = ((), (), s32[]{:S(2)}) async-start(), calls=%async_computation.2 | async-start | bytes 131072 | tf_op jit(solution)/shard_map/psum | solution.py:108
  235.1 72.6 %copy-start.1 = (f32[6144,128]{1,0:T(8,128)S(1)}, f32[6144,128]{1,0:T(8,128)}, u32[]{:S(2)}) copy-start(f32[6144,128]{1,0:T(8,128)} %copy.16) | copy-start | bytes 9437188
Sparse Core Ops, SparseCore 0:
  92.3 140.2 all-reduce.2
  235.0 65.1 all-reduce.4
